TPU v7x, 32 devices: a whole 2x2x4 slice. The times are simulated.
32 devices in a mesh: dp: 2 (over y), gx: 4 (over x, core), gy: 4 (over z).
Axes of the slice: x: 2, y: 2, z: 4, core: 2. Of those that a mesh axis runs over, the one named last changes fastest.
Arguments:
- tokens: bfloat16 [2, 11664, 1152], P(None, ('dp', 'gy'), 'gx'), may hold values from -6 to 6
- cotangent: bfloat16 [2, 11664, 1152], P(None, ('dp', 'gy'), 'gx'), may hold values from -6 to 6
- ln1_gain: bfloat16 [1152], P('gx'), may hold values from 0.25 to 1.75
- ln1_bias: bfloat16 [1152], P('gx'), may hold values from -3 to 3
- qkv_weight: bfloat16 [1152, 3, 1152], P('gx', None, 'gy'), may hold values from -0.1875 to 0.1875
- qv_bias: bfloat16 [2, 1152], P(None, 'gy'), may hold values from -3 to 3
- out_weight: bfloat16 [1152, 1152], P('gy', 'gx'), may hold values from -1.5 to 1.5
- out_bias: bfloat16 [1152], P('gx'), may hold values from -3 to 3
- ln2_gain: bfloat16 [1152], P('gx'), may hold values from 0.25 to 1.75
- ln2_bias: bfloat16 [1152], P('gx'), may hold values from -3 to 3
- fc1_weight: bfloat16 [1152, 4304], P('gx', 'gy'), may hold values from -0.1875 to 0.1875
- fc1_bias: bfloat16 [4304], P('gy'), may hold values from -3 to 3
- fc2_weight: bfloat16 [4304, 1152], P('gy', 'gx'), may hold values from -0.09375 to 0.09375
- fc2_bias: bfloat16 [1152], P('gx'), may hold values from -3 to 3
Outputs:
- layer_out: bfloat16 [2, 11664, 1152], P(None, ('dp', 'gy'), 'gx')
- tokens_grad: bfloat16 [2, 11664, 1152], P(None, ('dp', 'gy'), 'gx')
- ln1_gain_grad: float32 [1152], P('gx')
- ln1_bias_grad: float32 [1152], P('gx')
- qkv_weight_grad: float32 [1152, 3, 1152], P('gx', None, 'gy')
- qv_bias_grad: float32 [2, 1152], P(None, 'gy')
- out_weight_grad: float32 [1152, 1152], P('gy', 'gx')
- out_bias_grad: float32 [1152], P('gx')
- ln2_gain_grad: float32 [1152], P('gx')
- ln2_bias_grad: float32 [1152], P('gx')
- fc1_weight_grad: float32 [1152, 4304], P('gx', 'gy')
- fc1_bias_grad: float32 [4304], P('gy')
- fc2_weight_grad: float32 [4304, 1152], P('gy', 'gx')
- fc2_bias_grad: float32 [1152], P('gx')
All inputs are finite; a program needn't handle non-finite values.
Results may differ from a plain program's by a relative error of at most 0.013.
The roundings to bfloat16 on the way count: a program that leaves them out, or rounds other values in their place, can miss the bound.
Values may be sent and summed in bfloat16 or wider, within the bound.
No kernel may reach another device: no remote copies, remote signals or barrier semaphores. Data moves between devices by JAX's collectives and lax.ppermute only.
A program may use at most 384 MiB of HBM per device.

v0:
```python
import jax
import jax.numpy as jnp
from jax import lax
from jax.sharding import PartitionSpec as P

HEAD_DIM = 72
SEQ = 729
MICRO = 2
epsilon = 1e-06


def contract_rows(left_side, right_side):
    return lax.dot_general(
        left_side, right_side, (((0,), (0,)), ((), ())), preferred_element_type=jnp.float32
    )


def contract_cols(left_side, right_side):
    return lax.dot_general(
        left_side, right_side, (((1,), (1,)), ((), ())), preferred_element_type=jnp.float32
    )


def apply_weight(rows, weight, backward):
    if backward:
        return contract_cols(rows, weight)
    return jnp.dot(rows, weight, preferred_element_type=jnp.float32)


def gelu_tanh(values):
    return jax.nn.gelu(values, approximate=True)


def row_pair_sums(first_terms, second_terms):
    return lax.psum((jnp.sum(first_terms, axis=1), jnp.sum(second_terms, axis=1)), "gx")


def norm_forward(values):
    row_sum, row_square = row_pair_sums(values, values * values)
    full_width = values.shape[1] * lax.axis_size("gx")
    center = row_sum / full_width
    spread = row_square / full_width - center * center
    inverse = lax.rsqrt(spread + epsilon)
    return ((values - center[:, None]) * inverse[:, None], inverse)


def norm_backward(grad_norm, normed, inverse, norm_gain):
    grad_hat = grad_norm * norm_gain
    row_sum, row_cross = row_pair_sums(grad_hat, grad_hat * normed)
    full_width = grad_norm.shape[1] * lax.axis_size("gx")
    return inverse[:, None] * (
        grad_hat - row_sum[:, None] / full_width - normed * (row_cross[:, None] / full_width)
    )


def spread(row_block, weight, backward):
    gathered = lax.all_gather(row_block, "gy", axis=0, tiled=True)
    full_rows = lax.all_to_all(gathered, "gx", split_axis=0, concat_axis=1, tiled=True)
    if backward:
        whole_weight = lax.all_gather(weight, "gx", axis=1, tiled=True)
    else:
        whole_weight = lax.all_gather(weight, "gx", axis=0, tiled=True)
    return (gathered, apply_weight(full_rows, whole_weight, backward))


def join(row_block, weight, backward):
    gathered = lax.all_gather(row_block, "gx", axis=0, tiled=True)
    full_rows = lax.all_to_all(gathered, "gy", split_axis=0, concat_axis=1, tiled=True)
    if backward:
        whole_weight = lax.all_gather(weight, "gy", axis=1, tiled=True)
    else:
        whole_weight = lax.all_gather(weight, "gy", axis=0, tiled=True)
    return (gathered, apply_weight(full_rows, whole_weight, backward))


def attend_image(packed):
    queries = packed[:, 0]
    key_rows = packed[:, 1]
    values = packed[:, 2]
    scaling = queries.shape[-1] ** (-0.5)
    scores = (
        jnp.einsum("qhd,khd->hqk", queries, key_rows, preferred_element_type=jnp.float32) * scaling
    )
    row_max = jnp.max(scores, axis=2, keepdims=True)
    exponent = jnp.exp(scores - row_max)
    row_total = jnp.sum(exponent, axis=2, keepdims=True)
    probability = (exponent / row_total).astype(jnp.bfloat16)
    mixture = jnp.einsum("hqk,khd->qhd", probability, values, preferred_element_type=jnp.float32)
    return (mixture.astype(jnp.bfloat16), (row_max + jnp.log(row_total))[:, :, 0])


def attend_backward(element):
    packed, log_total, grad_mixture = element
    queries = packed[:, 0]
    key_rows = packed[:, 1]
    values = packed[:, 2]
    scaling = queries.shape[-1] ** (-0.5)
    scores = (
        jnp.einsum("qhd,khd->hqk", queries, key_rows, preferred_element_type=jnp.float32) * scaling
    )
    probability = jnp.exp(scores - log_total[:, :, None])
    rounded = probability.astype(jnp.bfloat16)
    grad_values = jnp.einsum(
        "hqk,qhd->khd", rounded, grad_mixture, preferred_element_type=jnp.float32
    )
    grad_prob = jnp.einsum("qhd,khd->hqk", grad_mixture, values, preferred_element_type=jnp.float32)
    inner_sum = jnp.sum(probability * grad_prob, axis=2, keepdims=True)
    grad_scores = (probability * (grad_prob - inner_sum)).astype(jnp.bfloat16)
    grad_queries = (
        jnp.einsum("hqk,khd->qhd", grad_scores, key_rows, preferred_element_type=jnp.float32)
        * scaling
    )
    grad_keys = (
        jnp.einsum("hqk,qhd->khd", grad_scores, queries, preferred_element_type=jnp.float32)
        * scaling
    )
    return jnp.stack([grad_queries, grad_keys, grad_values], axis=1).astype(jnp.bfloat16)


def total_grads(mat_grads, row_grads):
    mat_summed = lax.psum(
        (
            mat_grads[0],
            mat_grads[1],
            mat_grads[2],
            mat_grads[3],
            mat_grads[4],
            mat_grads[5],
            mat_grads[6],
            mat_grads[7],
        ),
        "dp",
    )
    row_summed = lax.psum((row_grads[0], row_grads[1], row_grads[2], row_grads[3]), ("dp", "gy"))
    return (mat_summed, row_summed)


def on_device(
    tokens,
    cotangent,
    ln1_gain,
    ln1_bias,
    qkv_weight,
    qv_bias,
    out_weight,
    out_bias,
    ln2_gain,
    ln2_bias,
    fc1_weight,
    fc1_bias,
    fc2_weight,
    fc2_bias,
):
    width_local = qkv_weight.shape[0]
    head_cols = qkv_weight.shape[2]
    heads_here = head_cols // HEAD_DIM
    qkv_flat = qkv_weight.reshape(width_local, 3 * head_cols)
    bias_rows = (
        jnp.stack([qv_bias[0], jnp.zeros_like(qv_bias[0]), qv_bias[1]])
        .astype(jnp.float32)
        .reshape(1, 3 * head_cols)
    )
    gain_one = ln1_gain.astype(jnp.float32)
    shift_one = ln1_bias.astype(jnp.float32)
    gain_two = ln2_gain.astype(jnp.float32)
    shift_two = ln2_bias.astype(jnp.float32)
    bias_mix = out_bias.astype(jnp.float32)
    bias_first = fc1_bias.astype(jnp.float32)
    bias_second = fc2_bias.astype(jnp.float32)
    outputs = []
    grad_inputs = []
    mat_total = None
    row_total = None
    for batch_index in range(MICRO):
        current = tokens[batch_index].astype(jnp.float32)
        normed_one, inverse_one = norm_forward(current)
        ready_one = (normed_one * gain_one + shift_one).astype(jnp.bfloat16)
        gathered_one, projected = spread(ready_one, qkv_flat, False)
        projected = projected + bias_rows
        attn_rows = projected.shape[0]
        picture_count = attn_rows // SEQ
        packed = projected.astype(jnp.bfloat16).reshape(picture_count, SEQ, 3, heads_here, HEAD_DIM)
        mixture, log_total = lax.map(attend_image, packed)
        mixture = mixture.reshape(attn_rows, head_cols)
        gathered_mix, attn_out = join(mixture, out_weight, False)
        hidden = current + attn_out + bias_mix
        normed_two, inverse_two = norm_forward(hidden)
        ready_two = (normed_two * gain_two + shift_two).astype(jnp.bfloat16)
        gathered_two, first_out = spread(ready_two, fc1_weight, False)
        active, gelu_pull = jax.vjp(gelu_tanh, first_out + bias_first)
        gathered_act, second_out = join(active.astype(jnp.bfloat16), fc2_weight, False)
        outputs.append((hidden + second_out + bias_second).astype(jnp.bfloat16))
        grad_out = cotangent[batch_index]
        grad_out_all, grad_active = spread(grad_out, fc2_weight, True)
        grad_fc2 = contract_rows(gathered_act, grad_out_all)
        grad_fc2_bias = jnp.sum(grad_out_all, axis=0, dtype=jnp.float32)
        grad_first = gelu_pull(grad_active)[0].astype(jnp.bfloat16)
        grad_first_all, grad_ready_two = join(grad_first, fc1_weight, True)
        grad_fc1 = contract_rows(gathered_two, grad_first_all)
        grad_fc1_bias = jnp.sum(grad_first_all, axis=0, dtype=jnp.float32)
        grad_gain_two = jnp.sum(grad_ready_two * normed_two, axis=0)
        grad_shift_two = jnp.sum(grad_ready_two, axis=0)
        grad_hidden = grad_out.astype(jnp.float32) + norm_backward(
            grad_ready_two, normed_two, inverse_two, gain_two
        )
        grad_hidden_all, grad_mixture = spread(grad_hidden.astype(jnp.bfloat16), out_weight, True)
        grad_out_weight = contract_rows(gathered_mix, grad_hidden_all)
        grad_out_bias = jnp.sum(grad_hidden_all, axis=0, dtype=jnp.float32)
        grad_mix_low = grad_mixture.astype(jnp.bfloat16).reshape(
            picture_count, SEQ, heads_here, HEAD_DIM
        )
        grad_packed = lax.map(attend_backward, (packed, log_total, grad_mix_low))
        grad_packed = grad_packed.reshape(attn_rows, 3 * head_cols)
        grad_packed_all, grad_ready_one = join(grad_packed, qkv_flat, True)
        grad_qkv = contract_rows(gathered_one, grad_packed_all).reshape(width_local, 3, head_cols)
        col_sums = jnp.sum(grad_packed_all, axis=0, dtype=jnp.float32).reshape(3, head_cols)
        grad_qv = jnp.stack([col_sums[0], col_sums[2]])
        grad_gain_one = jnp.sum(grad_ready_one * normed_one, axis=0)
        grad_shift_one = jnp.sum(grad_ready_one, axis=0)
        grad_inputs.append(
            (grad_hidden + norm_backward(grad_ready_one, normed_one, inverse_one, gain_one)).astype(
                jnp.bfloat16
            )
        )
        mat_grads = (
            grad_qkv,
            grad_qv,
            grad_out_weight,
            grad_out_bias,
            grad_fc1,
            grad_fc1_bias,
            grad_fc2,
            grad_fc2_bias,
        )
        row_grads = (grad_gain_one, grad_shift_one, grad_gain_two, grad_shift_two)
        mat_grads, row_grads = total_grads(mat_grads, row_grads)
        if batch_index == 0:
            mat_total, row_total = (mat_grads, row_grads)
        else:
            mat_total = jax.tree.map(jnp.add, mat_total, mat_grads)
            row_total = jax.tree.map(jnp.add, row_total, row_grads)
    return (
        jnp.stack(outputs),
        jnp.stack(grad_inputs),
        row_total[0],
        row_total[1],
        mat_total[0],
        mat_total[1],
        mat_total[2],
        mat_total[3],
        row_total[2],
        row_total[3],
        mat_total[4],
        mat_total[5],
        mat_total[6],
        mat_total[7],
    )


def solution(mesh):
    return jax.shard_map(
        on_device,
        mesh=mesh,
        in_specs=(
            P(None, ("dp", "gy"), "gx"),
            P(None, ("dp", "gy"), "gx"),
            P("gx"),
            P("gx"),
            P("gx", None, "gy"),
            P(None, "gy"),
            P("gy", "gx"),
            P("gx"),
            P("gx"),
            P("gx"),
            P("gx", "gy"),
            P("gy"),
            P("gy", "gx"),
            P("gx"),
        ),
        out_specs=(
            P(None, ("dp", "gy"), "gx"),
            P(None, ("dp", "gy"), "gx"),
            P("gx"),
            P("gx"),
            P("gx", None, "gy"),
            P(None, "gy"),
            P("gy", "gx"),
            P("gx"),
            P("gx"),
            P("gx"),
            P("gx", "gy"),
            P("gy"),
            P("gy", "gx"),
            P("gx"),
        ),
        check_vma=False,
    )
```

profile of v0, /device:TPU:0, one launch (start us, length us, event | category | flops | bytes accessed | tf_op | source)
XLA Modules:
  0.0 3569.1 jit_solution(3430166739071463660)
XLA Ops:
  11.1 12.9 all-reduce.4
  28.3 68.2 %all-gather.52.cloned.1.call-done = bf16[4,1458,288]{1,2,0:T(8,128)(2,1)} async-done(((bf16[1,1458,288]{1,2,0:T(8,128)(2,1)}), bf16[4,1458,288]{1,2,0:T(8,128)(2,1)}) %all-gather.52.cloned.1.call-update) | async-done | bytes 3359248 | tf_op jit(solution)/shard_map/all_gather | solution.py:57
  101.5 65.8 %all-gather.62.cloned.1.call-done = bf16[4,1458,288]{1,2,0:T(8,128)(2,1)} async-done(((bf16[1,1458,288]{1,2,0:T(8,128)(2,1)}), bf16[4,1458,288]{1,2,0:T(8,128)(2,1)}) %all-gather.62.cloned.1.call-update) | async-done | bytes 3359248 | tf_op jit(solution)/shard_map/all_gather | solution.py:57
  172.0 29.6 all-gather.42.cloned.1.call-done
  221.9 11.7 while.44
  247.3 9.5 reshape.380
  263.8 11.7 while.45
  285.7 26.1 all-gather.64.cloned.1.call-done
  311.8 53.7 %all-to-all-done.1 = bf16[4,1458,288]{1,2,0:T(8,128)(2,1)} async-done(((bf16[4,1458,288]{1,2,0:T(8,128)(2,1)}), bf16[4,1458,288]{1,2,0:T(8,128)(2,1)}, u32[]{:S(2)}, u32[]{:S(2)}) %all-to-all-start.1) | async-done | bytes 3359264 | tf_op jit(solution)/shard_map/all_to_all | solution.py:68
  379.5 187.2 %all_gather.83 = bf16[1152,288]{1,0:T(8,128)(2,1)S(1)} all-gather(bf16[288,288]{1,0:T(8,128)(2,1)} %param.28), channel_id=1, replica_groups=mesh['dp'=2,'gx'=4,'gy'=4] {'gy'}, dimensions={0}, use_global_device_ids=true | all-gather | bytes 829440 | tf_op jit(solution)/shard_map/all_gather | solution.py:72
  577.9 11.1 all-reduce.3
  607.9 38.1 %reduce.2 = bf16[5832,288]{1,0:T(8,128)(2,1)} reduce(bf16[1,5832,288]{2,0,1:T(2,128)(2,1)} %all-gather.48.cloned.1.call-done, bf16[]{:T(256)} %constant.107), dimensions={0}, to_apply=%all-gather.reduce_sub_computation | reduce | bytes 6718466 | tf_op jit(solution)/shard_map/all_gather | solution.py:57
  663.8 54.7 %all-to-all-done.8 = bf16[4,1458,288]{1,2,0:T(8,128)(2,1)} async-done(((bf16[4,1458,288]{1,2,0:T(8,128)(2,1)}), bf16[4,1458,288]{1,2,0:T(8,128)(2,1)}, u32[]{:S(2)}, u32[]{:S(2)}) %all-to-all-start.8) | async-done | bytes 3359264 | tf_op jit(solution)/shard_map/all_to_all | solution.py:58
  723.3 10.2 fusion.139
  733.6 26.0 all-gather.44.cloned.1.call-done
  759.6 19.1 all-to-all-done.2
  778.7 14.4 fusion.83
  793.1 126.9 %all-gather.50.cloned.1.call-done = bf16[1,5832,288]{2,0,1:T(2,128)(2,1)} async-done(((bf16[1,1458,288]{2,0,1:T(2,128)(2,1)}), bf16[1,5832,288]{2,0,1:T(2,128)(2,1)}) %all-gather.50.cloned.1.call-update) | async-done | bytes 3359248 | tf_op jit(solution)/shard_map/all_gather | solution.py:57
  920.0 38.1 %reduce.3 = bf16[5832,288]{1,0:T(8,128)(2,1)} reduce(bf16[1,5832,288]{2,0,1:T(2,128)(2,1)} %all-gather.50.cloned.1.call-done, bf16[]{:T(256)} %constant.107), dimensions={0}, to_apply=%all-gather.1.reduce_sub_computation | reduce | bytes 6718466 | tf_op jit(solution)/shard_map/all_gather | solution.py:57
  970.3 60.6 %all_to_all.304 = bf16[4,1458,288]{1,2,0:T(8,128)(2,1)} all-to-all(bf16[4,1458,288]{1,2,0:T(8,128)(2,1)} %copy.218), channel_id=1, replica_groups=mesh['dp'=2,'gx'=4,'gy'=4] {'gx'}, dimensions={0} | all-to-all | bytes 6718464 | tf_op jit(solution)/shard_map/all_to_all | solution.py:58
  1036.2 10.0 fusion.140
  1046.2 69.0 %all-to-all-done.6 = bf16[4,1458,288]{1,2,0:T(8,128)(2,1)} async-done(((bf16[4,1458,288]{1,2,0:T(8,128)(2,1)}), bf16[4,1458,288]{1,2,0:T(8,128)(2,1)}, u32[]{:S(2)}, u32[]{:S(2)}) %all-to-all-start.6) | async-done | bytes 3359264 | tf_op jit(solution)/shard_map/all_to_all | solution.py:58
  1115.2 14.1 fusion.82
  1136.2 76.6 %all-gather.80.cloned.1.call-done = bf16[4,1458,1076]{1,2,0:T(8,128)(2,1)} async-done(((bf16[1,1458,1076]{1,2,0:T(8,128)(2,1)}), bf16[4,1458,1076]{1,2,0:T(8,128)(2,1)}) %all-gather.80.cloned.1.call-update) | async-done | bytes 12550480 | tf_op jit(solution)/shard_map/all_gather | solution.py:67
  1212.8 210.8 %all-to-all-done.9 = bf16[4,1458,1076]{1,2,0:T(8,128)(2,1)} async-done(((bf16[4,1458,1076]{1,2,0:T(8,128)(2,1)}), bf16[4,1458,1076]{1,2,0:T(8,128)(2,1)}, u32[]{:S(2)}, u32[]{:S(2)}) %all-to-all-start.9) | async-done | bytes 12550496 | tf_op jit(solution)/shard_map/all_to_all | solution.py:68
  1430.9 138.4 %all-gather.72.cloned.1.call-done = bf16[4,1076,288]{1,2,0:T(8,128)(2,1)} async-done(((bf16[1,1076,288]{1,2,0:T(8,128)(2,1)}), bf16[4,1076,288]{1,2,0:T(8,128)(2,1)}) %all-gather.72.cloned.1.call-update) | async-done | bytes 2479120 | tf_op jit(solution)/shard_map/all_gather | solution.py:70
  1579.6 17.0 all_to_all.263
  1596.6 163.3 %all-to-all-done.13 = bf16[4,1458,1076]{1,2,0:T(8,128)(2,1)} async-done(((bf16[4,1458,1076]{1,2,0:T(8,128)(2,1)}), bf16[4,1458,1076]{1,2,0:T(8,128)(2,1)}, u32[]{:S(2)}, u32[]{:S(2)}) %all-to-all-start.13) | async-done | bytes 12550496 | tf_op jit(solution)/shard_map/all_to_all | solution.py:68
  1759.9 17.0 all_to_all.279
  1795.0 11.6 all-reduce.2
  1814.8 66.5 %all-gather.74.cloned.1.call-done = bf16[4,1458,288]{1,2,0:T(8,128)(2,1)} async-done(((bf16[1,1458,288]{1,2,0:T(8,128)(2,1)}), bf16[4,1458,288]{1,2,0:T(8,128)(2,1)}) %all-gather.74.cloned.1.call-update) | async-done | bytes 3359248 | tf_op jit(solution)/shard_map/all_gather | solution.py:57
  1885.1 114.2 %all-gather.58.cloned.1.call-done = bf16[4,1458,1076]{1,2,0:T(8,128)(2,1)} async-done(((bf16[1,1458,1076]{1,2,0:T(8,128)(2,1)}), bf16[4,1458,1076]{1,2,0:T(8,128)(2,1)}) %all-gather.58.cloned.1.call-update) | async-done | bytes 12550480 | tf_op jit(solution)/shard_map/all_gather | solution.py:67
  2025.3 59.5 %while.46 = (s32[]{:T(128)}, bf16[2,729,3,4,72]{1,4,3,2,0:T(8,128)(2,1)}, bf16[2,729,3,4,72]{1,4,3,2,0:T(8,128)(2,1)}, f32[2,4,729]{2,1,0:T(4,128)S(1)}, bf16[2,729,4,72]{1,3,2,0:T(8,128)(2,1)S(1)}, /*index=5*/s32[]{:T(128)}) while((s32[]{:T(128)}, bf16[2,729,3,4,72]{1,4,3,2,0:T(8,128)(2,1)}, bf16[2,729,3,4,72]{1,4,3,2,0:T(8,128)(2,1)}, ...), condition=%wide.region_30.31_spmd, body=%wide.region_28.30_spmd.sunk | while | flops 1560885248 | bytes 142425280 | solution.py:212
  2034.3 10.3 multiply_convert_fusion.6
  2064.1 10.2 multiply_convert_fusion.6
  2100.4 250.7 %all-to-all-done.3 = bf16[4,1458,1076]{1,2,0:T(8,128)(2,1)} async-done(((bf16[4,1458,1076]{1,2,0:T(8,128)(2,1)}), bf16[4,1458,1076]{1,2,0:T(8,128)(2,1)}, u32[]{:S(2)}, u32[]{:S(2)}) %all-to-all-start.3) | async-done | bytes 12550496 | tf_op jit(solution)/shard_map/all_to_all | solution.py:68
  2355.9 41.2 %all-to-all-done.14 = bf16[4,1458,288]{1,2,0:T(8,128)(2,1)} async-done(((bf16[4,1458,288]{1,2,0:T(8,128)(2,1)}), bf16[4,1458,288]{1,2,0:T(8,128)(2,1)}, u32[]{:S(2)}, u32[]{:S(2)}) %all-to-all-start.14) | async-done | bytes 3359264 | tf_op jit(solution)/shard_map/all_to_all | solution.py:58
  2411.6 59.4 %while.47 = (s32[]{:T(128)}, bf16[2,729,3,4,72]{1,4,3,2,0:T(8,128)(2,1)}, bf16[2,729,3,4,72]{1,4,3,2,0:T(8,128)(2,1)}, f32[2,4,729]{2,1,0:T(4,128)S(1)}, bf16[2,729,4,72]{1,3,2,0:T(8,128)(2,1)S(1)}, /*index=5*/s32[]{:T(128)}) while((s32[]{:T(128)}, bf16[2,729,3,4,72]{1,4,3,2,0:T(8,128)(2,1)}, bf16[2,729,3,4,72]{1,4,3,2,0:T(8,128)(2,1)}, ...), condition=%wide.region_41.42_spmd, body=%wide.region_39.41_spmd.sunk | while | flops 1560885248 | bytes 142425280 | solution.py:212
  2420.7 10.1 multiply_convert_fusion.7
  2450.4 10.1 multiply_convert_fusion.7
  2486.5 280.6 %all-to-all-done.7 = bf16[4,1458,1076]{1,2,0:T(8,128)(2,1)} async-done(((bf16[4,1458,1076]{1,2,0:T(8,128)(2,1)}), bf16[4,1458,1076]{1,2,0:T(8,128)(2,1)}, u32[]{:S(2)}, u32[]{:S(2)}) %all-to-all-start.7) | async-done | bytes 12550496 | tf_op jit(solution)/shard_map/all_to_all | solution.py:68
  2812.8 19.3 copy.238
  2832.1 20.9 copy.236
  2904.1 41.9 %copy.232 = bf16[4,1458,1076]{1,0,2:T(4,128)(2,1)} copy(bf16[4,1458,1076]{1,2,0:T(8,128)(2,1)} %all-gather.70.cloned.1.call-done) | data formatting | bytes 25100928 | tf_op jit(solution)/shard_map/all_gather | solution.py:67
  2946.0 25.3 reshape.342
  2971.3 41.8 %copy.234 = bf16[4,1458,1076]{1,0,2:T(4,128)(2,1)} copy(bf16[4,1458,1076]{1,2,0:T(8,128)(2,1)} %all-gather.80.cloned.1.call-done) | data formatting | bytes 25100928 | tf_op jit(solution)/shard_map/all_gather | solution.py:67
  3013.2 25.5 reshape.352
  3038.7 41.8 %copy.235 = bf16[4,1458,1076]{1,0,2:T(4,128)(2,1)} copy(bf16[4,1458,1076]{1,2,0:T(8,128)(2,1)} %all-gather.58.cloned.1.call-done) | data formatting | bytes 25100928 | tf_op jit(solution)/shard_map/all_gather | solution.py:67
  3080.5 25.3 reshape.330
  3105.8 41.8 %copy.237 = bf16[4,1458,1076]{1,0,2:T(4,128)(2,1)} copy(bf16[4,1458,1076]{1,2,0:T(8,128)(2,1)} %all-gather.68.cloned.1.call-done) | data formatting | bytes 25100928 | tf_op jit(solution)/shard_map/all_gather | solution.py:67
  3147.6 25.3 reshape.340
  3200.4 10.4 fusion.145
  3220.1 11.3 convolution_add_fusion.2
  3231.4 17.1 all_to_all.239
  3248.6 17.4 all_to_all.255
  3267.2 10.6 fusion.94
  3307.9 14.4 reshape.348
  3322.3 14.8 reshape.356
  3350.5 9.7 fusion.93
  3381.0 84.2 %all-reduce.9.cloned.1.call-done = (f32[288,3,288]{0,2,1:T(8,128)}, f32[288,288]{1,0:T(8,128)}, f32[288,1076]{1,0:T(8,128)}, f32[1076,288]{0,1:T(8,128)}) async-done(((f32[288,3,288]{0,2,1:T(8,128)}, f32[288,288]{1,0:T(8,128)}, f32[288,1076]{1,0:T(8,128)}, f32[1076,288]{0,1:T(8,128)}), (f32[288,3,288]{0,2,1:T(8,128)}, f32[288,288]{1,0:T(8,128)}, f32[288,1076]{1,0:T(8,128)}, ...) | async-done | bytes 3806224 | tf_op jit(solution)/shard_map/psum | solution.py:121
  3468.1 14.5 copy.213
  3482.6 14.5 copy.223
  3512.8 12.6 all-reduce.1
  3537.6 21.7 all-reduce
  (503 shorter events, 616.5 us)
Async XLA Ops:
  7.2 89.3 %all-gather.52.cloned.1.call-start = ((), (), s32[]{:S(2)}) async-start(), calls=%async_computation.21 | async-start | bytes 4423680 | tf_op jit(solution)/shard_map/all_gather | solution.py:57
  9.1 17.7 copy-start.52
  26.0 141.2 %all-gather.62.cloned.1.call-start = ((), (), s32[]{:S(2)}) async-start(), calls=%async_computation.26 | async-start | bytes 4423680 | tf_op jit(solution)/shard_map/all_gather | solution.py:57
  26.8 174.8 %all-gather.42.cloned.1.call-start = ((), (), s32[]{:S(2)}) async-start(), calls=%async_computation.16 | async-start | bytes 2580480 | tf_op jit(solution)/shard_map/all_gather | solution.py:62
  27.2 69.3 %copy-start.36 = (bf16[288,3,288]{0,2,1:T(8,128)(2,1)}, bf16[288,3,288]{0,2,1:T(8,128)(2,1)S(1)}, u32[]{:S(2)}) copy-start(bf16[288,3,288]{0,2,1:T(8,128)(2,1)S(1)} %copy.195) | copy-start | bytes 1492996
  28.3 73.0 %copy-start.96 = (bf16[2,288]{1,0:T(2,128)(2,1)S(1)}, bf16[2,288]{1,0:T(2,128)(2,1)}, u32[]{:S(2)}) copy-start(bf16[2,288]{1,0:T(2,128)(2,1)} %param.27) | copy-start | bytes 3460
  96.5 70.8 %all-to-all-start = ((bf16[4,1458,288]{1,2,0:T(8,128)(2,1)}), bf16[4,1458,288]{1,2,0:T(8,128)(2,1)}, u32[]{:S(2)}, u32[]{:S(2)}) async-start(bf16[4,1458,288]{1,2,0:T(8,128)(2,1)} %all-gather.52.cloned.1.call-done), calls=%async_computation | async-start | bytes 7077888 | tf_op jit(solution)/shard_map/all_to_all | solution.py:58
  167.3 71.7 %all-to-all-start.4 = ((bf16[4,1458,288]{1,2,0:T(8,128)(2,1)}), bf16[4,1458,288]{1,2,0:T(8,128)(2,1)}, u32[]{:S(2)}, u32[]{:S(2)}) async-start(bf16[4,1458,288]{1,2,0:T(8,128)(2,1)} %all-gather.62.cloned.1.call-done), calls=%async_computation.4 | async-start | bytes 7077888 | tf_op jit(solution)/shard_map/all_to_all | solution.py:58
  172.0 108.9 %all-gather.54.cloned.1.call-start = ((), (), s32[]{:S(2)}) async-start(), calls=%async_computation.22 | async-start | bytes 4423680 | tf_op jit(solution)/shard_map/all_gather | solution.py:67
  238.9 72.9 %all-gather.64.cloned.1.call-start = ((), (), s32[]{:S(2)}) async-start(), calls=%async_computation.27 | async-start | bytes 4423680 | tf_op jit(solution)/shard_map/all_gather | solution.py:67
  280.9 84.6 %all-to-all-start.1 = ((bf16[4,1458,288]{1,2,0:T(8,128)(2,1)}), bf16[4,1458,288]{1,2,0:T(8,128)(2,1)}, u32[]{:S(2)}, u32[]{:S(2)}) async-start(bf16[4,1458,288]{1,2,0:T(8,128)(2,1)} %all-gather.54.cloned.1.call-done), calls=%async_computation.1 | async-start | bytes 7077888 | tf_op jit(solution)/shard_map/all_to_all | solution.py:68
  285.7 84.6 %copy-start.10 = (bf16[2,1458,288]{1,2,0:T(8,128)(2,1)S(1)}, bf16[2,1458,288]{1,2,0:T(8,128)(2,1)}, u32[]{:S(2)}) copy-start(bf16[2,1458,288]{1,2,0:T(8,128)(2,1)} %param.23) | copy-start | bytes 5038852
  365.5 206.8 %all-to-all-start.5 = ((bf16[4,1458,288]{1,2,0:T(8,128)(2,1)}), bf16[4,1458,288]{1,2,0:T(8,128)(2,1)}, u32[]{:S(2)}, u32[]{:S(2)}) async-start(bf16[4,1458,288]{1,2,0:T(8,128)(2,1)} %all-gather.64.cloned.1.call-done), calls=%async_computation.5 | async-start | bytes 7077888 | tf_op jit(solution)/shard_map/all_to_all | solution.py:68
  370.2 237.6 %all-gather.48.cloned.1.call-start = ((), (), s32[]{:S(2)}) async-start(), calls=%async_computation.19 | async-start | bytes 11197440 | tf_op jit(solution)/shard_map/all_gather | solution.py:57
  371.6 195.9 %copy-start.8 = (bf16[2,1458,288]{1,2,0:T(8,128)(2,1)S(1)}, bf16[2,1458,288]{1,2,0:T(8,128)(2,1)}, u32[]{:S(2)}) copy-start(bf16[2,1458,288]{1,2,0:T(8,128)(2,1)} %param.22) | copy-start | bytes 5038852
  378.2 340.3 %all-gather.56.cloned.1.call-start = ((), (), s32[]{:S(2)}) async-start(), calls=%async_computation.23 | async-start | bytes 4423680 | tf_op jit(solution)/shard_map/all_gather | solution.py:57
  378.3 188.4 %copy-start.103 = (f32[288]{0:T(512)}, f32[288]{0:T(512)S(1)}, u32[]{:S(2)}) copy-start(f32[288]{0:T(512)S(1)} %convert_element_type.181) | copy-start | bytes 3460
  589.0 1219.0 %copy-start.60 = (f32[1458]{0:T(1024)}, f32[1458]{0:T(1024)S(1)}, u32[]{:S(2)}) copy-start(f32[1458]{0:T(1024)S(1)} %get-tuple-element.374) | copy-start | bytes 17500
  589.0 1219.0 %copy-start.62 = (f32[1458]{0:T(1024)}, f32[1458]{0:T(1024)S(1)}, u32[]{:S(2)}) copy-start(f32[1458]{0:T(1024)S(1)} %get-tuple-element.375) | copy-start | bytes 17500
  593.1 130.3 %all-gather.46.cloned.1.call-start = ((), (), s32[]{:S(2)}) async-start(), calls=%async_computation.18 | async-start | bytes 3317760 | tf_op jit(solution)/shard_map/all_gather | solution.py:60
  593.9 165.7 %all-gather.44.cloned.1.call-start = ((), (), s32[]{:S(2)}) async-start(), calls=%async_computation.17 | async-start | bytes 3317760 | tf_op jit(solution)/shard_map/all_gather | solution.py:62
  594.6 325.4 %all-gather.50.cloned.1.call-start = ((), (), s32[]{:S(2)}) async-start(), calls=%async_computation.20 | async-start | bytes 11197440 | tf_op jit(solution)/shard_map/all_gather | solution.py:57
  658.3 60.2 %all-to-all-start.8 = ((bf16[4,1458,288]{1,2,0:T(8,128)(2,1)}), bf16[4,1458,288]{1,2,0:T(8,128)(2,1)}, u32[]{:S(2)}, u32[]{:S(2)}) async-start(bf16[4,1458,288]{1,2,0:T(8,128)(2,1)} %copy.206), calls=%async_computation.8 | async-start | bytes 7077888 | tf_op jit(solution)/shard_map/all_to_all | solution.py:58
  663.0 367.9 %all-gather.66.cloned.1.call-start = ((), (), s32[]{:S(2)}) async-start(), calls=%async_computation.28 | async-start | bytes 4423680 | tf_op jit(solution)/shard_map/all_gather | solution.py:57
  663.8 59.5 %copy-start.97 = (bf16[1076]{0:T(1024)(128)(2,1)S(1)}, bf16[1076]{0:T(1024)(128)(2,1)}, u32[]{:S(2)}) copy-start(bf16[1076]{0:T(1024)(128)(2,1)} %param.33) | copy-start | bytes 6460
  718.5 60.2 %all-to-all-start.2 = ((bf16[4,1458,288]{1,2,0:T(8,128)(2,1)}), bf16[4,1458,288]{1,2,0:T(8,128)(2,1)}, u32[]{:S(2)}, u32[]{:S(2)}) async-start(bf16[4,1458,288]{1,2,0:T(8,128)(2,1)} %all-gather.56.cloned.1.call-done), calls=%async_computation.2 | async-start | bytes 7077888 | tf_op jit(solution)/shard_map/all_to_all | solution.py:58
  723.2 406.1 %all-gather.70.cloned.1.call-start = ((), (), s32[]{:S(2)}) async-start(), calls=%async_computation.30 | async-start | bytes 16588800 | tf_op jit(solution)/shard_map/all_gather | solution.py:67
  1030.9 84.2 %all-to-all-start.6 = ((bf16[4,1458,288]{1,2,0:T(8,128)(2,1)}), bf16[4,1458,288]{1,2,0:T(8,128)(2,1)}, u32[]{:S(2)}, u32[]{:S(2)}) async-start(bf16[4,1458,288]{1,2,0:T(8,128)(2,1)} %all-gather.66.cloned.1.call-done), calls=%async_computation.6 | async-start | bytes 7077888 | tf_op jit(solution)/shard_map/all_to_all | solution.py:58
  1035.7 177.1 %all-gather.80.cloned.1.call-start = ((), (), s32[]{:S(2)}) async-start(), calls=%async_computation.35 | async-start | bytes 16588800 | tf_op jit(solution)/shard_map/all_gather | solution.py:67
  1129.4 294.2 %all-to-all-start.9 = ((bf16[4,1458,1076]{1,2,0:T(8,128)(2,1)}), bf16[4,1458,1076]{1,2,0:T(8,128)(2,1)}, u32[]{:S(2)}, u32[]{:S(2)}) async-start(bf16[4,1458,1076]{1,2,0:T(8,128)(2,1)} %all-gather.70.cloned.1.call-done), calls=%async_computation.9 | async-start | bytes 26542080 | tf_op jit(solution)/shard_map/all_to_all | solution.py:68
  1423.6 336.3 %all-to-all-start.13 = ((bf16[4,1458,1076]{1,2,0:T(8,128)(2,1)}), bf16[4,1458,1076]{1,2,0:T(8,128)(2,1)}, u32[]{:S(2)}, u32[]{:S(2)}) async-start(bf16[4,1458,1076]{1,2,0:T(8,128)(2,1)} %all-gather.80.cloned.1.call-done), calls=%async_computation.13 | async-start | bytes 26542080 | tf_op jit(solution)/shard_map/all_to_all | solution.py:68
  1430.1 139.2 %all-gather.72.cloned.1.call-start = ((), (), s32[]{:S(2)}) async-start(), calls=%async_computation.31 | async-start | bytes 3317760 | tf_op jit(solution)/shard_map/all_gather | solution.py:70
  1430.6 450.7 %all-gather.74.cloned.1.call-start = ((), (), s32[]{:S(2)}) async-start(), calls=%async_computation.32 | async-start | bytes 4423680 | tf_op jit(solution)/shard_map/all_gather | solution.py:57
  1813.0 186.2 %all-gather.58.cloned.1.call-start = ((), (), s32[]{:S(2)}) async-start(), calls=%async_computation.24 | async-start | bytes 16588800 | tf_op jit(solution)/shard_map/all_gather | solution.py:67
  1813.6 537.5 %all-gather.82.cloned.1.call-start = ((), (), s32[]{:S(2)}) async-start(), calls=%async_computation.36 | async-start | bytes 4423680 | tf_op jit(solution)/shard_map/all_gather | solution.py:57
  1814.2 541.7 %all-gather.68.cloned.1.call-start = ((), (), s32[]{:S(2)}) async-start(), calls=%async_computation.29 | async-start | bytes 16588800 | tf_op jit(solution)/shard_map/all_gather | solution.py:67
  1881.3 118.0 %all-to-all-start.10 = ((bf16[4,1458,288]{1,2,0:T(8,128)(2,1)}), bf16[4,1458,288]{1,2,0:T(8,128)(2,1)S(1)}, u32[]{:S(2)}, u32[]{:S(2)}) async-start(bf16[4,1458,288]{1,2,0:T(8,128)(2,1)} %all-gather.74.cloned.1.call-done), calls=%async_computation.10 | async-start | bytes 7077888 | tf_op jit(solution)/shard_map/all_to_all | solution.py:58
  1999.3 351.8 %all-to-all-start.3 = ((bf16[4,1458,1076]{1,2,0:T(8,128)(2,1)}), bf16[4,1458,1076]{1,2,0:T(8,128)(2,1)}, u32[]{:S(2)}, u32[]{:S(2)}) async-start(bf16[4,1458,1076]{1,2,0:T(8,128)(2,1)} %all-gather.58.cloned.1.call-done), calls=%async_computation.3 | async-start | bytes 26542080 | tf_op jit(solution)/shard_map/all_to_all | solution.py:68
  2005.8 761.4 %all-gather.76.cloned.1.call-start = ((), (), s32[]{:S(2)}) async-start(), calls=%async_computation.33 | async-start | bytes 13117440 | tf_op jit(solution)/shard_map/all_gather | solution.py:67
  2351.1 46.0 %all-to-all-start.14 = ((bf16[4,1458,288]{1,2,0:T(8,128)(2,1)}), bf16[4,1458,288]{1,2,0:T(8,128)(2,1)}, u32[]{:S(2)}, u32[]{:S(2)}) async-start(bf16[4,1458,288]{1,2,0:T(8,128)(2,1)} %all-gather.82.cloned.1.call-done), calls=%async_computation.14 | async-start | bytes 7077888 | tf_op jit(solution)/shard_map/all_to_all | solution.py:58
  2355.8 47.7 %copy-start.37 = (bf16[288,3,288]{0,2,1:T(8,128)(2,1)S(1)}, bf16[288,3,288]{0,2,1:T(8,128)(2,1)}, u32[]{:S(2)}) copy-start(bf16[288,3,288]{0,2,1:T(8,128)(2,1)} %copy-done.36) | copy-start | bytes 1492996
  2355.9 49.8 %copy-start.50 = (bf16[288,1152]{0,1:T(8,128)(2,1)S(1)}, bf16[288,1152]{0,1:T(8,128)(2,1)}, u32[]{:S(2)}) copy-start(bf16[288,1152]{0,1:T(8,128)(2,1)} %copy-done.49) | copy-start | bytes 1990660
  2397.1 370.1 %all-to-all-start.7 = ((bf16[4,1458,1076]{1,2,0:T(8,128)(2,1)}), bf16[4,1458,1076]{1,2,0:T(8,128)(2,1)}, u32[]{:S(2)}, u32[]{:S(2)}) async-start(bf16[4,1458,1076]{1,2,0:T(8,128)(2,1)} %all-gather.68.cloned.1.call-done), calls=%async_computation.7 | async-start | bytes 26542080 | tf_op jit(solution)/shard_map/all_to_all | solution.py:68
  2403.5 370.5 %all-gather.78.cloned.1.call-start = ((), (), s32[]{:S(2)}) async-start(), calls=%async_computation.34 | async-start | bytes 2580480 | tf_op jit(solution)/shard_map/all_gather | solution.py:70
  2404.7 374.7 %all-gather.60.cloned.1.call-start = ((), (), s32[]{:S(2)}) async-start(), calls=%async_computation.25 | async-start | bytes 3317760 | tf_op jit(solution)/shard_map/all_gather | solution.py:72
  2405.4 767.5 %all-gather.84.cloned.1.call-start = ((), (), s32[]{:S(2)}) async-start(), calls=%async_computation.37 | async-start | bytes 13117440 | tf_op jit(solution)/shard_map/all_gather | solution.py:67
  2486.5 286.9 %copy-start.109 = (bf16[288]{0:T(512)(128)(2,1)S(1)}, bf16[288]{0:T(512)(128)(2,1)}, u32[]{:S(2)}) copy-start(bf16[288]{0:T(512)(128)(2,1)} %param.35) | copy-start | bytes 1732
  2767.2 405.8 %all-to-all-start.11 = ((bf16[4,1458,864]{2,1,0:T(8,128)(2,1)}), bf16[4,1458,864]{2,1,0:T(8,128)(2,1)}, u32[]{:S(2)}, u32[]{:S(2)}) async-start(bf16[4,1458,864]{2,1,0:T(8,128)(2,1)} %all-gather.76.cloned.1.call-done), calls=%async_computation.11 | async-start | bytes 20987904 | tf_op jit(solution)/shard_map/all_to_all | solution.py:68
  3172.9 309.7 %all-to-all-start.15 = ((bf16[4,1458,864]{2,1,0:T(8,128)(2,1)}), bf16[4,1458,864]{2,1,0:T(8,128)(2,1)}, u32[]{:S(2)}, u32[]{:S(2)}) async-start(bf16[4,1458,864]{2,1,0:T(8,128)(2,1)} %all-gather.84.cloned.1.call-done), calls=%async_computation.15 | async-start | bytes 20987904 | tf_op jit(solution)/shard_map/all_to_all | solution.py:68
  3179.0 286.2 %all-reduce.9.cloned.1.call-start = ((), (), s32[]{:S(2)}) async-start(), calls=%async_computation.38 | async-start | bytes 8847360 | tf_op jit(solution)/shard_map/psum | solution.py:121
  3248.5 17.5 copy-start.100
  3248.5 17.5 copy-start.101
  3248.5 18.1 copy-start.98
  3248.5 18.1 copy-start.99
  3248.5 18.7 copy-start.13
  3248.5 18.6 copy-start.102
  3350.5 19.7 slice-start
  3350.5 19.7 slice-start.1
  3506.5 24.3 copy-start.11
  3506.5 24.3 copy-start.66
  3506.5 24.3 copy-start.69
  3536.2 23.1 copy-start.53
  3536.2 23.8 copy-start.47
  3536.3 24.9 copy-start.46
  (95 other events, 558.3 us)
Sparse Core Ops, SparseCore 0:
  26.2 70.3 all-gather.51
  98.6 68.5 all-gather.61
  169.4 32.1 all-gather.41
  239.0 30.7 all-gather.53
  281.0 30.7 all-gather.63
  378.3 229.4 all-gather.47
  610.0 68.0 all-gather.55
  679.6 38.6 all-gather.45
  719.9 39.6 all-gather.43
  761.0 158.9 all-gather.49
  922.1 68.1 all-gather.65
  991.8 136.1 all-gather.69
  1129.5 83.2 all-gather.79
  1432.2 137.0 all-gather.71
  1813.2 68.1 all-gather.73
  1882.7 116.4 all-gather.57
  2001.3 166.1 all-gather.81
  2168.9 83.2 all-gather.67
  2253.8 70.2 all-gather.75
  2406.2 122.8 all-gather.77
  2530.7 91.3 all-gather.59
  2623.7 163.8 all-gather.83
  3350.5 114.6 all-reduce.8
where the time goes:
time: 3590 us; the launch traced here: 3570 us
  waiting for transfers between devices  1980 us (55%)
  local copies, waits for them, and re-layouts  705 us (20%)
  blocking collectives  336 us (9%)
  matrix products  263 us (7%)
  other arithmetic  187 us (5%)
  starting transfers between devices  82.3 us (2%)
    all_to_all x8, waiting for transfers between devices, join(): lax.all_to_all(gathered, 'gy', split_axis=0, concat_axis=1, tiled=True)  959 us
    all_gather x8, waiting for transfers between devices, spread(): gathered = lax.all_gather(row_block, 'gy', axis=0, tiled=True)  336 us
    unnamed x240, local copies, waits for them, and re-layouts  258 us
    all_gather x8, waiting for transfers between devices, join(): gathered = lax.all_gather(row_block, 'gx', axis=0, tiled=True)  217 us
    all_gather x1, blocking collectives, join(): whole_weight = lax.all_gather(weight, 'gy', axis=0, tiled=True)  187 us
    all_to_all x7, waiting for transfers between devices, spread(): lax.all_to_all(gathered, 'gx', split_axis=0, concat_axis=1, tiled=True)  184 us
    all_gather x6, local copies, waits for them, and re-layouts, join(): gathered = lax.all_gather(row_block, 'gx', axis=0, tiled=True)  176 us
    all_gather x2, waiting for transfers between devices, join(): whole_weight = lax.all_gather(weight, 'gy', axis=1, tiled=True)  138 us
  transfers between devices with their start and end apart: 38, of which 21 were waited for; matrix products, arithmetic and copies ran while one was open for 28% of the time, Pallas kernels for 0%

commit v1 on v0

--- a/solution.py
+++ b/solution.py
@@ -7,6 +7,28 @@
 SEQ = 729
 MICRO = 2
 epsilon = 1e-06
+
+
+def cut_along(value, dim, devices):
+    before, after = (value.shape[:dim], value.shape[dim + 1 :])
+    return jnp.moveaxis(value.reshape(*before, devices, -1, *after), dim, 0)
+
+
+def in_order(parts, dim):
+    shape = list(parts.shape[1:])
+    shape[dim] *= parts.shape[0]
+    return jnp.moveaxis(parts, 0, dim).reshape(shape)
+
+
+def swapped_with_each(array, axis, split_dim, concat_dim):
+    peers, index = (lax.axis_size(axis), lax.axis_index(axis))
+    parts = cut_along(array, split_dim, peers)
+    outs = [parts[index]]
+    for hop in range(1, peers):
+        sent = parts[index ^ hop]
+        outs.append(lax.ppermute(sent, axis, [(i, i ^ hop) for i in range(peers)]))
+    parts = jnp.stack(outs)[index ^ jnp.arange(peers)]
+    return in_order(parts, concat_dim)
 
 
 def contract_rows(left_side, right_side):
@@ -55,7 +77,7 @@
 
 def spread(row_block, weight, backward):
     gathered = lax.all_gather(row_block, "gy", axis=0, tiled=True)
-    full_rows = lax.all_to_all(gathered, "gx", split_axis=0, concat_axis=1, tiled=True)
+    full_rows = swapped_with_each(gathered, "gx", 0, 1)
     if backward:
         whole_weight = lax.all_gather(weight, "gx", axis=1, tiled=True)
     else:

time: 3590 us -> 3350 us (0.933)
  waiting for transfers between devices: 1980 us -> 1790 us
  other arithmetic: 187 us -> 124 us
  local copies, waits for them, and re-layouts: 705 us -> 760 us
    ppermute x0 -> x24, waiting for transfers between devices: none -> 270 us  [swapped_with_each(): outs.append(lax.ppermute(sent, axis, [(i, i ^ hop) for i in range(peers)]))]
    all_to_all x8, waiting for transfers between devices: 959 us -> 754 us  [join(): lax.all_to_all(gathered, 'gy', split_axis=0, concat_axis=1, tiled=True)]
    all_to_all x7 -> x0, waiting for transfers between devices: 184 us -> none  [spread(): lax.all_to_all(gathered, 'gx', split_axis=0, concat_axis=1, tiled=True)]
    all_gather x8, waiting for transfers between devices: 217 us -> 117 us  [join(): gathered = lax.all_gather(row_block, 'gx', axis=0, tiled=True)]
    all_gather x2 -> x0, other arithmetic: 76.3 us -> none  [spread(): gathered = lax.all_gather(row_block, 'gy', axis=0, tiled=True)]
    all_gather x1, blocking collectives: 9.36 us -> 82.9 us  [spread(): whole_weight = lax.all_gather(weight, 'gx', axis=1, tiled=True)]
    all_gather x8, waiting for transfers between devices: 336 us -> 403 us  [spread(): gathered = lax.all_gather(row_block, 'gy', axis=0, tiled=True)]
    all_to_all x1 -> x0, blocking collectives: 60.6 us -> none  [spread(): lax.all_to_all(gathered, 'gx', split_axis=0, concat_axis=1, tiled=True)]
  transfers between devices with their start and end apart: 38 -> 55, of which waited for: 21 -> 26; matrix products, arithmetic and copies ran while one was open for 28% -> 30% of each run, Pallas kernels for 0% -> 0%
where the time goes in v1:
time: 3350 us; the launch traced here: 3340 us
  waiting for transfers between devices  1790 us (53%)
  local copies, waits for them, and re-layouts  760 us (23%)
  blocking collectives  320 us (10%)
  matrix products  260 us (8%)
  other arithmetic  124 us (4%)
  starting transfers between devices  67.1 us (2%)
    all_to_all x8, waiting for transfers between devices, join(): lax.all_to_all(gathered, 'gy', split_axis=0, concat_axis=1, tiled=True)  754 us
    all_gather x8, waiting for transfers between devices, spread(): gathered = lax.all_gather(row_block, 'gy', axis=0, tiled=True)  403 us
    ppermute x24, waiting for transfers between devices, swapped_with_each(): outs.append(lax.ppermute(sent, axis, [(i, i ^ hop) for i in range(peers)]))  270 us
    unnamed x270, local copies, waits for them, and re-layouts  259 us
    all_gather x6, local copies, waits for them, and re-layouts, join(): gathered = lax.all_gather(row_block, 'gx', axis=0, tiled=True)  180 us
    all_gather x1, blocking collectives, join(): whole_weight = lax.all_gather(weight, 'gy', axis=0, tiled=True)  159 us
    all_gather x2, waiting for transfers between devices, join(): whole_weight = lax.all_gather(weight, 'gy', axis=1, tiled=True)  138 us
    all_gather x8, waiting for transfers between devices, join(): gathered = lax.all_gather(row_block, 'gx', axis=0, tiled=True)  117 us
  transfers between devices with their start and end apart: 55, of which 26 were waited for; matrix products, arithmetic and copies ran while one was open for 30% of the time, Pallas kernels for 0%

profile of v1, /device:TPU:0, one launch (start us, length us, event | category | flops | bytes accessed | tf_op | source)
XLA Modules:
  0.0 3340.2 jit_solution(10832000872825968341)
XLA Ops:
  11.1 12.9 all-reduce.4
  28.7 67.8 %all-gather.52.cloned.1.call-done = bf16[4,1458,288]{1,2,0:T(8,128)(2,1)} async-done(((bf16[1,1458,288]{1,2,0:T(8,128)(2,1)}), bf16[4,1458,288]{1,2,0:T(8,128)(2,1)}) %all-gather.52.cloned.1.call-update) | async-done | bytes 3359248 | tf_op jit(solution)/shard_map/all_gather | solution.py:79
  102.1 65.2 %all-gather.62.cloned.1.call-done = bf16[4,1458,288]{1,2,0:T(8,128)(2,1)} async-done(((bf16[1,1458,288]{1,2,0:T(8,128)(2,1)}), bf16[4,1458,288]{1,2,0:T(8,128)(2,1)}) %all-gather.62.cloned.1.call-update) | async-done | bytes 3359248 | tf_op jit(solution)/shard_map/all_gather | solution.py:79
  179.0 22.0 all-gather.42.cloned.1.call-done
  221.0 12.2 while.44
  267.2 11.9 while.45
  295.5 20.3 all-gather.64.cloned.1.call-done
  315.9 114.8 %all-to-all-done = bf16[4,1458,288]{1,2,0:T(8,128)(2,1)} async-done(((bf16[4,1458,288]{1,2,0:T(8,128)(2,1)}), bf16[4,1458,288]{1,2,0:T(8,128)(2,1)}, u32[]{:S(2)}, u32[]{:S(2)}) %all-to-all-start) | async-done | bytes 3359264 | tf_op jit(solution)/shard_map/all_to_all | solution.py:90
  441.3 159.0 %all_gather.83 = bf16[1152,288]{1,0:T(8,128)(2,1)S(1)} all-gather(bf16[288,288]{1,0:T(8,128)(2,1)S(1)} %copy-done.60), channel_id=1, replica_groups=mesh['dp'=2,'gx'=4,'gy'=4] {'gy'}, dimensions={0}, use_global_device_ids=true | all-gather | bytes 829440 | tf_op jit(solution)/shard_map/all_gather | solution.py:94
  611.0 10.7 all-reduce.3
  626.6 19.3 copy.156
  652.8 109.9 %all-gather.50.cloned.1.call-done = bf16[1,5832,288]{2,0,1:T(2,128)(2,1)} async-done(((bf16[1,1458,288]{2,0,1:T(2,128)(2,1)}), bf16[1,5832,288]{2,0,1:T(2,128)(2,1)}) %all-gather.50.cloned.1.call-update) | async-done | bytes 3359248 | tf_op jit(solution)/shard_map/all_gather | solution.py:79
  762.7 19.3 copy.168
  790.3 19.1 constant_dynamic-slice_fusion.4
  812.6 19.7 collective-permute-done.13
  832.3 26.5 collective-permute-done.14
  877.2 25.7 collective-permute-done.4
  902.9 18.5 collective-permute-done.5
  926.0 14.3 fusion.83
  945.4 20.4 collective-permute-done.19
  965.7 17.4 collective-permute-done.20
  998.5 32.3 collective-permute-done.10
  1030.8 37.3 %collective-permute-done.11 = bf16[1458,288]{0,1:T(8,128)(2,1)S(1)} collective-permute-done((bf16[1458,288]{0,1:T(8,128)(2,1)S(1)}, bf16[1458,288]{0,1:T(8,128)(2,1)S(1)}, u32[]{:S(2)}, u32[]{:S(2)}) %collective-permute-start.11) | collective-permute-done | bytes 839840 | tf_op jit(solution)/shard_map/ppermute | solution.py:29
  1071.3 14.1 fusion.82
  1085.4 18.0 all-gather.70.cloned.1.call-done
  1109.9 78.4 %all-gather.80.cloned.1.call-done = bf16[4,1458,1076]{1,2,0:T(8,128)(2,1)} async-done(((bf16[1,1458,1076]{1,2,0:T(8,128)(2,1)}), bf16[4,1458,1076]{1,2,0:T(8,128)(2,1)}) %all-gather.80.cloned.1.call-update) | async-done | bytes 12550480 | tf_op jit(solution)/shard_map/all_gather | solution.py:89
  1188.3 210.0 %all-to-all-done.4 = bf16[4,1458,1076]{1,2,0:T(8,128)(2,1)} async-done(((bf16[4,1458,1076]{1,2,0:T(8,128)(2,1)}), bf16[4,1458,1076]{1,2,0:T(8,128)(2,1)}, u32[]{:S(2)}, u32[]{:S(2)}) %all-to-all-start.4) | async-done | bytes 12550496 | tf_op jit(solution)/shard_map/all_to_all | solution.py:90
  1405.9 138.4 %all-gather.72.cloned.1.call-done = bf16[4,1076,288]{1,2,0:T(8,128)(2,1)} async-done(((bf16[1,1076,288]{1,2,0:T(8,128)(2,1)}), bf16[4,1076,288]{1,2,0:T(8,128)(2,1)}) %all-gather.72.cloned.1.call-update) | async-done | bytes 2479120 | tf_op jit(solution)/shard_map/all_gather | solution.py:92
  1550.8 18.2 all_to_all.131
  1569.0 165.9 %all-to-all-done.6 = bf16[4,1458,1076]{1,2,0:T(8,128)(2,1)} async-done(((bf16[4,1458,1076]{1,2,0:T(8,128)(2,1)}), bf16[4,1458,1076]{1,2,0:T(8,128)(2,1)}, u32[]{:S(2)}, u32[]{:S(2)}) %all-to-all-start.6) | async-done | bytes 12550496 | tf_op jit(solution)/shard_map/all_to_all | solution.py:90
  1735.0 17.1 all_to_all.139
  1770.2 11.5 all-reduce.2
  1796.6 160.2 %all-gather.74.cloned.1.call-done = bf16[4,1458,288]{1,2,0:T(8,128)(2,1)} async-done(((bf16[1,1458,288]{1,2,0:T(8,128)(2,1)}), bf16[4,1458,288]{1,2,0:T(8,128)(2,1)}) %all-gather.74.cloned.1.call-update) | async-done | bytes 3359248 | tf_op jit(solution)/shard_map/all_gather | solution.py:79
  1962.6 82.9 %all_gather.97 = bf16[288,1152]{0,1:T(8,128)(2,1)} all-gather(bf16[288,288]{0,1:T(8,128)(2,1)S(1)} %copy.159), channel_id=1, replica_groups=mesh['dp'=2,'gx'=4,'gy'=4] {'gx'}, dimensions={1}, use_global_device_ids=true | all-gather | bytes 829440 | tf_op jit(solution)/shard_map/all_gather | solution.py:82
  2058.4 59.7 %while.46 = (s32[]{:T(128)}, bf16[2,729,3,4,72]{1,4,3,2,0:T(8,128)(2,1)}, bf16[2,729,3,4,72]{1,4,3,2,0:T(8,128)(2,1)}, f32[2,4,729]{2,1,0:T(4,128)S(1)}, bf16[2,729,4,72]{1,3,2,0:T(8,128)(2,1)S(1)}, /*index=5*/s32[]{:T(128)}) while((s32[]{:T(128)}, bf16[2,729,3,4,72]{1,4,3,2,0:T(8,128)(2,1)}, bf16[2,729,3,4,72]{1,4,3,2,0:T(8,128)(2,1)}, ...), condition=%wide.region_30.31_spmd, body=%wide.region_28.30_spmd.sunk | while | flops 1560885248 | bytes 142425280 | solution.py:234
  2067.3 10.3 multiply_convert_fusion.6
  2097.3 10.2 multiply_convert_fusion.6
  2133.6 65.1 %all-to-all-done.1 = bf16[4,1458,1076]{1,2,0:T(8,128)(2,1)} async-done(((bf16[4,1458,1076]{1,2,0:T(8,128)(2,1)}), bf16[4,1458,1076]{1,2,0:T(8,128)(2,1)}, u32[]{:S(2)}, u32[]{:S(2)}) %all-to-all-start.1) | async-done | bytes 12550496 | tf_op jit(solution)/shard_map/all_to_all | solution.py:90
  2212.8 39.0 %collective-permute-done.22 = bf16[1458,288]{0,1:T(8,128)(2,1)S(1)} collective-permute-done((bf16[1458,288]{0,1:T(8,128)(2,1)}, bf16[1458,288]{0,1:T(8,128)(2,1)S(1)}, u32[]{:S(2)}, u32[]{:S(2)}) %collective-permute-start.22) | collective-permute-done | bytes 839840 | tf_op jit(solution)/shard_map/ppermute | solution.py:29
  2251.8 32.7 collective-permute-done.23
  2296.8 59.5 %while.47 = (s32[]{:T(128)}, bf16[2,729,3,4,72]{1,4,3,2,0:T(8,128)(2,1)}, bf16[2,729,3,4,72]{1,4,3,2,0:T(8,128)(2,1)}, f32[2,4,729]{2,1,0:T(4,128)S(1)}, bf16[2,729,4,72]{1,3,2,0:T(8,128)(2,1)S(1)}, /*index=5*/s32[]{:T(128)}) while((s32[]{:T(128)}, bf16[2,729,3,4,72]{1,4,3,2,0:T(8,128)(2,1)}, bf16[2,729,3,4,72]{1,4,3,2,0:T(8,128)(2,1)}, ...), condition=%wide.region_41.42_spmd, body=%wide.region_39.41_spmd.sunk | while | flops 1560885248 | bytes 142425280 | solution.py:234
  2305.8 10.3 multiply_convert_fusion.7
  2335.6 10.2 multiply_convert_fusion.7
  2371.8 197.9 %all-to-all-done.3 = bf16[4,1458,1076]{1,2,0:T(8,128)(2,1)} async-done(((bf16[4,1458,1076]{1,2,0:T(8,128)(2,1)}), bf16[4,1458,1076]{1,2,0:T(8,128)(2,1)}, u32[]{:S(2)}, u32[]{:S(2)}) %all-to-all-start.3) | async-done | bytes 12550496 | tf_op jit(solution)/shard_map/all_to_all | solution.py:90
  2673.1 41.8 %copy.183 = bf16[4,1458,1076]{1,0,2:T(4,128)(2,1)} copy(bf16[4,1458,1076]{1,2,0:T(8,128)(2,1)} %all-gather.70.cloned.1.call-done) | data formatting | bytes 25100928 | tf_op jit(solution)/shard_map/all_gather | solution.py:89
  2715.0 25.3 reshape.462
  2740.3 41.8 %copy.185 = bf16[4,1458,1076]{1,0,2:T(4,128)(2,1)} copy(bf16[4,1458,1076]{1,2,0:T(8,128)(2,1)} %all-gather.80.cloned.1.call-done) | data formatting | bytes 25100928 | tf_op jit(solution)/shard_map/all_gather | solution.py:89
  2782.1 25.7 reshape.472
  2807.8 41.8 %copy.186 = bf16[4,1458,1076]{1,0,2:T(4,128)(2,1)} copy(bf16[4,1458,1076]{1,2,0:T(8,128)(2,1)} %all-gather.58.cloned.1.call-done) | data formatting | bytes 25100928 | tf_op jit(solution)/shard_map/all_gather | solution.py:89
  2849.7 25.3 reshape.450
  2875.0 41.8 %copy.188 = bf16[4,1458,1076]{1,0,2:T(4,128)(2,1)} copy(bf16[4,1458,1076]{1,2,0:T(8,128)(2,1)} %all-gather.68.cloned.1.call-done) | data formatting | bytes 25100928 | tf_op jit(solution)/shard_map/all_gather | solution.py:89
  2916.9 25.3 reshape.460
  2971.5 10.2 fusion.146
  2991.0 11.3 convolution_add_fusion.2
  3002.3 17.1 all_to_all.119
  3019.4 17.6 all_to_all.127
  3038.1 10.6 fusion.94
  3078.7 14.5 reshape.468
  3093.2 15.1 reshape.476
  3152.2 84.2 %all-reduce.9.cloned.1.call-done = (f32[288,3,288]{0,2,1:T(8,128)}, f32[288,288]{1,0:T(8,128)}, f32[288,1076]{1,0:T(8,128)}, f32[1076,288]{0,1:T(8,128)}) async-done(((f32[288,3,288]{0,2,1:T(8,128)}, f32[288,288]{1,0:T(8,128)}, f32[288,1076]{1,0:T(8,128)}, f32[1076,288]{0,1:T(8,128)}), (f32[288,3,288]{0,2,1:T(8,128)}, f32[288,288]{1,0:T(8,128)}, f32[288,1076]{1,0:T(8,128)}, ...) | async-done | bytes 3806224 | tf_op jit(solution)/shard_map/psum | solution.py:143
  3239.3 14.6 copy.164
  3254.0 14.4 copy.174
  3284.1 12.6 all-reduce.1
  3308.9 21.6 all-reduce
  (589 shorter events, 667.3 us)
Async XLA Ops:
  7.2 89.3 %all-gather.52.cloned.1.call-start = ((), (), s32[]{:S(2)}) async-start(), calls=%async_computation.13 | async-start | bytes 4423680 | tf_op jit(solution)/shard_map/all_gather | solution.py:79
  26.0 141.2 %all-gather.62.cloned.1.call-start = ((), (), s32[]{:S(2)}) async-start(), calls=%async_computation.18 | async-start | bytes 4423680 | tf_op jit(solution)/shard_map/all_gather | solution.py:79
  26.8 174.2 %all-gather.42.cloned.1.call-start = ((), (), s32[]{:S(2)}) async-start(), calls=%async_computation.8 | async-start | bytes 2580480 | tf_op jit(solution)/shard_map/all_gather | solution.py:84
  27.2 72.8 %copy-start.34 = (bf16[288,3,288]{0,2,1:T(8,128)(2,1)}, bf16[288,3,288]{0,2,1:T(8,128)(2,1)S(1)}, u32[]{:S(2)}) copy-start(bf16[288,3,288]{0,2,1:T(8,128)(2,1)S(1)} %copy.146) | copy-start | bytes 1492996
  28.3 256.2 %all-gather.54.cloned.1.call-start = ((), (), s32[]{:S(2)}) async-start(), calls=%async_computation.14 | async-start | bytes 4423680 | tf_op jit(solution)/shard_map/all_gather | solution.py:89
  28.7 73.2 %copy-start.107 = (bf16[2,288]{1,0:T(2,128)(2,1)S(1)}, bf16[2,288]{1,0:T(2,128)(2,1)}, u32[]{:S(2)}) copy-start(bf16[2,288]{1,0:T(2,128)(2,1)} %param.27) | copy-start | bytes 3460
  100.0 72.6 %collective-permute-start = (bf16[1458,288]{0,1:T(8,128)(2,1)}, bf16[1458,288]{0,1:T(8,128)(2,1)S(1)}, u32[]{:S(2)}, u32[]{:S(2)}) collective-permute-start(bf16[1458,288]{0,1:T(8,128)(2,1)} %get-tuple-element.361), channel_id=1, source_target_pairs={{0,4},{4,0},{8,12},{12,8},{1,5},{5,1},{9,13},{13,9},{2,6},{6,2},{1... | collective-permute-start | bytes 2519432 | tf_op jit(solution)/shard_map/ppermute | solution.py:29
  100.0 73.0 %collective-permute-start.1 = (bf16[1458,288]{0,1:T(8,128)(2,1)}, bf16[1458,288]{0,1:T(8,128)(2,1)S(1)}, u32[]{:S(2)}, u32[]{:S(2)}) collective-permute-start(bf16[1458,288]{0,1:T(8,128)(2,1)} %get-tuple-element.363), channel_id=1, source_target_pairs={{0,8},{4,12},{8,0},{12,4},{1,9},{5,13},{9,1},{13,5},{2,10},{6,14},... | collective-permute-start | bytes 2519432 | tf_op jit(solution)/shard_map/ppermute | solution.py:29
  101.6 71.5 %collective-permute-start.2 = (bf16[1458,288]{0,1:T(8,128)(2,1)S(1)}, bf16[1458,288]{0,1:T(8,128)(2,1)S(1)}, u32[]{:S(2)}, u32[]{:S(2)}) collective-permute-start(bf16[1458,288]{0,1:T(8,128)(2,1)S(1)} %get-tuple-element.362), channel_id=1, source_target_pairs={{0,12},{4,8},{8,4},{12,0},{1,13},{5,9},{9,5},{13,1},{2,14},{6,10},... | collective-permute-start | bytes 2519432 | tf_op jit(solution)/shard_map/ppermute | solution.py:29
  102.1 140.2 %copy-start.101 = (s32[1024]{0:T(1024)}, s32[1024]{0:T(1024)S(1)}, u32[]{:S(2)}) copy-start(s32[1024]{0:T(1024)S(1)} %pad_clamp_fusion) | copy-start | bytes 12292
  171.2 67.4 %collective-permute-start.6 = (bf16[1458,288]{0,1:T(8,128)(2,1)}, bf16[1458,288]{0,1:T(8,128)(2,1)}, u32[]{:S(2)}, u32[]{:S(2)}) collective-permute-start(bf16[1458,288]{0,1:T(8,128)(2,1)} %get-tuple-element.365), channel_id=1, source_target_pairs={{0,4},{4,0},{8,12},{12,8},{1,5},{5,1},{9,13},{13,9},{2,6},{6,2},{1... | collective-permute-start | bytes 2519432 | tf_op jit(solution)/shard_map/ppermute | solution.py:29
  171.2 67.5 %collective-permute-start.7 = (bf16[1458,288]{0,1:T(8,128)(2,1)}, bf16[1458,288]{0,1:T(8,128)(2,1)}, u32[]{:S(2)}, u32[]{:S(2)}) collective-permute-start(bf16[1458,288]{0,1:T(8,128)(2,1)} %get-tuple-element.367), channel_id=1, source_target_pairs={{0,8},{4,12},{8,0},{12,4},{1,9},{5,13},{9,1},{13,5},{2,10},{6,14},... | collective-permute-start | bytes 2519432 | tf_op jit(solution)/shard_map/ppermute | solution.py:29
  172.6 66.0 %collective-permute-start.8 = (bf16[1458,288]{0,1:T(8,128)(2,1)}, bf16[1458,288]{0,1:T(8,128)(2,1)}, u32[]{:S(2)}, u32[]{:S(2)}) collective-permute-start(bf16[1458,288]{0,1:T(8,128)(2,1)} %get-tuple-element.366), channel_id=1, source_target_pairs={{0,12},{4,8},{8,4},{12,0},{1,13},{5,9},{9,5},{13,1},{2,14},{6,10},... | collective-permute-start | bytes 2519432 | tf_op jit(solution)/shard_map/ppermute | solution.py:29
  238.5 77.3 %all-gather.64.cloned.1.call-start = ((), (), s32[]{:S(2)}) async-start(), calls=%async_computation.19 | async-start | bytes 4423680 | tf_op jit(solution)/shard_map/all_gather | solution.py:89
  284.5 146.1 %all-to-all-start = ((bf16[4,1458,288]{1,2,0:T(8,128)(2,1)}), bf16[4,1458,288]{1,2,0:T(8,128)(2,1)}, u32[]{:S(2)}, u32[]{:S(2)}) async-start(bf16[4,1458,288]{1,2,0:T(8,128)(2,1)} %all-gather.54.cloned.1.call-done), calls=%async_computation | async-start | bytes 7077888 | tf_op jit(solution)/shard_map/all_to_all | solution.py:90
  289.4 337.2 %all-gather.48.cloned.1.call-start = ((), (), s32[]{:S(2)}) async-start(), calls=%async_computation.11 | async-start | bytes 11197440 | tf_op jit(solution)/shard_map/all_gather | solution.py:79
  430.7 174.1 %all-to-all-start.2 = ((bf16[4,1458,288]{1,2,0:T(8,128)(2,1)}), bf16[4,1458,288]{1,2,0:T(8,128)(2,1)}, u32[]{:S(2)}, u32[]{:S(2)}) async-start(bf16[4,1458,288]{1,2,0:T(8,128)(2,1)} %all-gather.64.cloned.1.call-done), calls=%async_computation.2 | async-start | bytes 7077888 | tf_op jit(solution)/shard_map/all_to_all | solution.py:90
  435.4 165.8 %copy-start.9 = (bf16[2,1458,288]{1,2,0:T(8,128)(2,1)S(1)}, bf16[2,1458,288]{1,2,0:T(8,128)(2,1)}, u32[]{:S(2)}) copy-start(bf16[2,1458,288]{1,2,0:T(8,128)(2,1)} %param.22) | copy-start | bytes 5038852
  435.4 327.3 %all-gather.50.cloned.1.call-start = ((), (), s32[]{:S(2)}) async-start(), calls=%async_computation.12 | async-start | bytes 11197440 | tf_op jit(solution)/shard_map/all_gather | solution.py:79
  440.0 422.0 %all-gather.56.cloned.1.call-start = ((), (), s32[]{:S(2)}) async-start(), calls=%async_computation.15 | async-start | bytes 4423680 | tf_op jit(solution)/shard_map/all_gather | solution.py:79
  440.1 160.2 %copy-start.113 = (f32[288]{0:T(512)}, f32[288]{0:T(512)S(1)}, u32[]{:S(2)}) copy-start(f32[288]{0:T(512)S(1)} %convert_element_type.181) | copy-start | bytes 3460
  621.7 1162.8 %copy-start.70 = (f32[1458]{0:T(1024)}, f32[1458]{0:T(1024)S(1)}, u32[]{:S(2)}) copy-start(f32[1458]{0:T(1024)S(1)} %get-tuple-element.374) | copy-start | bytes 17500
  621.7 1162.7 %copy-start.72 = (f32[1458]{0:T(1024)}, f32[1458]{0:T(1024)S(1)}, u32[]{:S(2)}) copy-start(f32[1458]{0:T(1024)S(1)} %get-tuple-element.375) | copy-start | bytes 17500
  625.2 243.5 %all-gather.46.cloned.1.call-start = ((), (), s32[]{:S(2)}) async-start(), calls=%async_computation.10 | async-start | bytes 3317760 | tf_op jit(solution)/shard_map/all_gather | solution.py:82
  625.9 300.1 %all-gather.44.cloned.1.call-start = ((), (), s32[]{:S(2)}) async-start(), calls=%async_computation.9 | async-start | bytes 3317760 | tf_op jit(solution)/shard_map/all_gather | solution.py:84
  626.5 359.7 %all-gather.66.cloned.1.call-start = ((), (), s32[]{:S(2)}) async-start(), calls=%async_computation.20 | async-start | bytes 4423680 | tf_op jit(solution)/shard_map/all_gather | solution.py:79
  790.2 313.2 %all-gather.70.cloned.1.call-start = ((), (), s32[]{:S(2)}) async-start(), calls=%async_computation.22 | async-start | bytes 16588800 | tf_op jit(solution)/shard_map/all_gather | solution.py:89
  809.5 3.0 collective-permute-start.12
  809.8 22.5 collective-permute-start.13
  811.4 47.4 %collective-permute-start.14 = (bf16[1458,288]{0,1:T(8,128)(2,1)S(1)}, bf16[1458,288]{0,1:T(8,128)(2,1)S(1)}, u32[]{:S(2)}, u32[]{:S(2)}) collective-permute-start(bf16[1458,288]{0,1:T(8,128)(2,1)S(1)} %bitcast.598), channel_id=1, source_target_pairs={{0,12},{4,8},{8,4},{12,0},{1,13},{5,9},{9,5},{13,1},{2,14},{6,10},... | collective-permute-start | bytes 2519432 | tf_op jit(solution)/shard_map/ppermute | solution.py:29
  866.0 11.1 collective-permute-start.3
  866.1 36.7 %collective-permute-start.4 = (bf16[1458,288]{0,1:T(8,128)(2,1)}, bf16[1458,288]{0,1:T(8,128)(2,1)}, u32[]{:S(2)}, u32[]{:S(2)}) collective-permute-start(bf16[1458,288]{0,1:T(8,128)(2,1)} %get-tuple-element.355), channel_id=1, source_target_pairs={{0,8},{4,12},{8,0},{12,4},{1,9},{5,13},{9,1},{13,5},{2,10},{6,14},... | collective-permute-start | bytes 2519432 | tf_op jit(solution)/shard_map/ppermute | solution.py:29
  868.7 52.7 %collective-permute-start.5 = (bf16[1458,288]{0,1:T(8,128)(2,1)}, bf16[1458,288]{0,1:T(8,128)(2,1)}, u32[]{:S(2)}, u32[]{:S(2)}) collective-permute-start(bf16[1458,288]{0,1:T(8,128)(2,1)} %get-tuple-element.354), channel_id=1, source_target_pairs={{0,12},{4,8},{8,4},{12,0},{1,13},{5,9},{9,5},{13,1},{2,14},{6,10},... | collective-permute-start | bytes 2519432 | tf_op jit(solution)/shard_map/ppermute | solution.py:29
  940.4 247.9 %all-gather.80.cloned.1.call-start = ((), (), s32[]{:S(2)}) async-start(), calls=%async_computation.27 | async-start | bytes 16588800 | tf_op jit(solution)/shard_map/all_gather | solution.py:89
  942.2 3.2 collective-permute-start.18
  943.2 22.6 collective-permute-start.19
  945.1 38.0 %collective-permute-start.20 = (bf16[1458,288]{0,1:T(8,128)(2,1)S(1)}, bf16[1458,288]{0,1:T(8,128)(2,1)S(1)}, u32[]{:S(2)}, u32[]{:S(2)}) collective-permute-start(bf16[1458,288]{0,1:T(8,128)(2,1)S(1)} %bitcast.599), channel_id=1, source_target_pairs={{0,12},{4,8},{8,4},{12,0},{1,13},{5,9},{9,5},{13,1},{2,14},{6,10},... | collective-permute-start | bytes 2519432 | tf_op jit(solution)/shard_map/ppermute | solution.py:29
  989.2 9.3 collective-permute-start.9
  989.8 41.0 %collective-permute-start.10 = (bf16[1458,288]{0,1:T(8,128)(2,1)S(1)}, bf16[1458,288]{0,1:T(8,128)(2,1)S(1)}, u32[]{:S(2)}, u32[]{:S(2)}) collective-permute-start(bf16[1458,288]{0,1:T(8,128)(2,1)S(1)} %get-tuple-element.359), channel_id=1, source_target_pairs={{0,8},{4,12},{8,0},{12,4},{1,9},{5,13},{9,1},{13,5},{2,10},{6,14},... | collective-permute-start | bytes 2519432 | tf_op jit(solution)/shard_map/ppermute | solution.py:29
  991.6 76.5 %collective-permute-start.11 = (bf16[1458,288]{0,1:T(8,128)(2,1)S(1)}, bf16[1458,288]{0,1:T(8,128)(2,1)S(1)}, u32[]{:S(2)}, u32[]{:S(2)}) collective-permute-start(bf16[1458,288]{0,1:T(8,128)(2,1)S(1)} %get-tuple-element.358), channel_id=1, source_target_pairs={{0,12},{4,8},{8,4},{12,0},{1,13},{5,9},{9,5},{13,1},{2,14},{6,10},... | collective-permute-start | bytes 2519432 | tf_op jit(solution)/shard_map/ppermute | solution.py:29
  1103.5 294.8 %all-to-all-start.4 = ((bf16[4,1458,1076]{1,2,0:T(8,128)(2,1)}), bf16[4,1458,1076]{1,2,0:T(8,128)(2,1)}, u32[]{:S(2)}, u32[]{:S(2)}) async-start(bf16[4,1458,1076]{1,2,0:T(8,128)(2,1)} %all-gather.70.cloned.1.call-done), calls=%async_computation.4 | async-start | bytes 26542080 | tf_op jit(solution)/shard_map/all_to_all | solution.py:90
  1398.3 336.7 %all-to-all-start.6 = ((bf16[4,1458,1076]{1,2,0:T(8,128)(2,1)}), bf16[4,1458,1076]{1,2,0:T(8,128)(2,1)}, u32[]{:S(2)}, u32[]{:S(2)}) async-start(bf16[4,1458,1076]{1,2,0:T(8,128)(2,1)} %all-gather.80.cloned.1.call-done), calls=%async_computation.6 | async-start | bytes 26542080 | tf_op jit(solution)/shard_map/all_to_all | solution.py:90
  1404.7 139.6 %all-gather.72.cloned.1.call-start = ((), (), s32[]{:S(2)}) async-start(), calls=%async_computation.23 | async-start | bytes 3317760 | tf_op jit(solution)/shard_map/all_gather | solution.py:92
  1405.3 384.8 %all-gather.58.cloned.1.call-start = ((), (), s32[]{:S(2)}) async-start(), calls=%async_computation.16 | async-start | bytes 16588800 | tf_op jit(solution)/shard_map/all_gather | solution.py:89
  1405.9 550.9 %all-gather.74.cloned.1.call-start = ((), (), s32[]{:S(2)}) async-start(), calls=%async_computation.24 | async-start | bytes 4423680 | tf_op jit(solution)/shard_map/all_gather | solution.py:79
  1789.5 344.1 %all-gather.68.cloned.1.call-start = ((), (), s32[]{:S(2)}) async-start(), calls=%async_computation.21 | async-start | bytes 16588800 | tf_op jit(solution)/shard_map/all_gather | solution.py:89
  1790.1 408.6 %all-to-all-start.1 = ((bf16[4,1458,1076]{1,2,0:T(8,128)(2,1)}), bf16[4,1458,1076]{1,2,0:T(8,128)(2,1)}, u32[]{:S(2)}, u32[]{:S(2)}) async-start(bf16[4,1458,1076]{1,2,0:T(8,128)(2,1)} %all-gather.58.cloned.1.call-done), calls=%async_computation.1 | async-start | bytes 26542080 | tf_op jit(solution)/shard_map/all_to_all | solution.py:90
  1796.5 165.9 %copy-start.61 = (bf16[288,288]{1,0:T(8,128)(2,1)S(1)}, bf16[288,288]{1,0:T(8,128)(2,1)}, u32[]{:S(2)}) copy-start(bf16[288,288]{1,0:T(8,128)(2,1)} %param.28) | copy-start | bytes 497668
  1796.5 410.1 %all-gather.82.cloned.1.call-start = ((), (), s32[]{:S(2)}) async-start(), calls=%async_computation.28 | async-start | bytes 4423680 | tf_op jit(solution)/shard_map/all_gather | solution.py:79
  1960.6 85.0 %collective-permute-start.15 = (bf16[1458,288]{0,1:T(8,128)(2,1)}, bf16[1458,288]{0,1:T(8,128)(2,1)S(1)}, u32[]{:S(2)}, u32[]{:S(2)}) collective-permute-start(bf16[1458,288]{0,1:T(8,128)(2,1)} %get-tuple-element.337), channel_id=1, source_target_pairs={{0,4},{4,0},{8,12},{12,8},{1,5},{5,1},{9,13},{13,9},{2,6},{6,2},{1... | collective-permute-start | bytes 2519432 | tf_op jit(solution)/shard_map/ppermute | solution.py:29
  1960.6 85.0 %collective-permute-start.16 = (bf16[1458,288]{0,1:T(8,128)(2,1)}, bf16[1458,288]{0,1:T(8,128)(2,1)S(1)}, u32[]{:S(2)}, u32[]{:S(2)}) collective-permute-start(bf16[1458,288]{0,1:T(8,128)(2,1)} %get-tuple-element.339), channel_id=1, source_target_pairs={{0,8},{4,12},{8,0},{12,4},{1,9},{5,13},{9,1},{13,5},{2,10},{6,14},... | collective-permute-start | bytes 2519432 | tf_op jit(solution)/shard_map/ppermute | solution.py:29
  1962.0 83.6 %collective-permute-start.17 = (bf16[1458,288]{0,1:T(8,128)(2,1)}, bf16[1458,288]{0,1:T(8,128)(2,1)S(1)}, u32[]{:S(2)}, u32[]{:S(2)}) collective-permute-start(bf16[1458,288]{0,1:T(8,128)(2,1)} %get-tuple-element.338), channel_id=1, source_target_pairs={{0,12},{4,8},{8,4},{12,0},{1,13},{5,9},{9,5},{13,1},{2,14},{6,10},... | collective-permute-start | bytes 2519432 | tf_op jit(solution)/shard_map/ppermute | solution.py:29
  2045.5 524.2 %all-gather.76.cloned.1.call-start = ((), (), s32[]{:S(2)}) async-start(), calls=%async_computation.25 | async-start | bytes 13117440 | tf_op jit(solution)/shard_map/all_gather | solution.py:89
  2198.7 371.0 %all-to-all-start.3 = ((bf16[4,1458,1076]{1,2,0:T(8,128)(2,1)}), bf16[4,1458,1076]{1,2,0:T(8,128)(2,1)}, u32[]{:S(2)}, u32[]{:S(2)}) async-start(bf16[4,1458,1076]{1,2,0:T(8,128)(2,1)} %all-gather.68.cloned.1.call-done), calls=%async_computation.3 | async-start | bytes 26542080 | tf_op jit(solution)/shard_map/all_to_all | solution.py:90
  2205.1 370.9 %all-gather.78.cloned.1.call-start = ((), (), s32[]{:S(2)}) async-start(), calls=%async_computation.26 | async-start | bytes 2580480 | tf_op jit(solution)/shard_map/all_gather | solution.py:92
  2206.5 375.0 %all-gather.60.cloned.1.call-start = ((), (), s32[]{:S(2)}) async-start(), calls=%async_computation.17 | async-start | bytes 3317760 | tf_op jit(solution)/shard_map/all_gather | solution.py:94
  2210.1 2.6 collective-permute-start.21
  2210.2 41.7 %collective-permute-start.22 = (bf16[1458,288]{0,1:T(8,128)(2,1)}, bf16[1458,288]{0,1:T(8,128)(2,1)S(1)}, u32[]{:S(2)}, u32[]{:S(2)}) collective-permute-start(bf16[1458,288]{0,1:T(8,128)(2,1)} %get-tuple-element.343), channel_id=1, source_target_pairs={{0,8},{4,12},{8,0},{12,4},{1,9},{5,13},{9,1},{13,5},{2,10},{6,14},... | collective-permute-start | bytes 2519432 | tf_op jit(solution)/shard_map/ppermute | solution.py:29
  2211.1 73.5 %collective-permute-start.23 = (bf16[1458,288]{0,1:T(8,128)(2,1)S(1)}, bf16[1458,288]{0,1:T(8,128)(2,1)S(1)}, u32[]{:S(2)}, u32[]{:S(2)}) collective-permute-start(bf16[1458,288]{0,1:T(8,128)(2,1)S(1)} %get-tuple-element.342), channel_id=1, source_target_pairs={{0,12},{4,8},{8,4},{12,0},{1,13},{5,9},{9,5},{13,1},{2,14},{6,10},... | collective-permute-start | bytes 2519432 | tf_op jit(solution)/shard_map/ppermute | solution.py:29
  2212.0 730.2 %all-gather.84.cloned.1.call-start = ((), (), s32[]{:S(2)}) async-start(), calls=%async_computation.29 | async-start | bytes 13117440 | tf_op jit(solution)/shard_map/all_gather | solution.py:89
  2371.8 204.3 %copy-start.119 = (bf16[288]{0:T(512)(128)(2,1)S(1)}, bf16[288]{0:T(512)(128)(2,1)}, u32[]{:S(2)}) copy-start(bf16[288]{0:T(512)(128)(2,1)} %param.35) | copy-start | bytes 1732
  2569.7 372.5 %all-to-all-start.5 = ((bf16[4,1458,864]{2,1,0:T(8,128)(2,1)}), bf16[4,1458,864]{2,1,0:T(8,128)(2,1)}, u32[]{:S(2)}, u32[]{:S(2)}) async-start(bf16[4,1458,864]{2,1,0:T(8,128)(2,1)} %all-gather.76.cloned.1.call-done), calls=%async_computation.5 | async-start | bytes 20987904 | tf_op jit(solution)/shard_map/all_to_all | solution.py:90
  2942.2 311.8 %all-to-all-start.7 = ((bf16[4,1458,864]{2,1,0:T(8,128)(2,1)}), bf16[4,1458,864]{2,1,0:T(8,128)(2,1)}, u32[]{:S(2)}, u32[]{:S(2)}) async-start(bf16[4,1458,864]{2,1,0:T(8,128)(2,1)} %all-gather.84.cloned.1.call-done), calls=%async_computation.7 | async-start | bytes 20987904 | tf_op jit(solution)/shard_map/all_to_all | solution.py:90
  2948.2 288.2 %all-reduce.9.cloned.1.call-start = ((), (), s32[]{:S(2)}) async-start(), calls=%async_computation.30 | async-start | bytes 8847360 | tf_op jit(solution)/shard_map/psum | solution.py:143
  (123 other events, 1106.9 us)
Sparse Core Ops, SparseCore 0:
  26.2 70.3 all-gather.51
  98.6 68.5 all-gather.61
  168.8 32.1 all-gather.41
  238.7 30.7 all-gather.53
  284.6 31.2 all-gather.63
  317.3 286.3 all-gather.47
  605.3 157.4 all-gather.49
  764.9 68.1 all-gather.55
  834.7 31.8 all-gather.45
  868.0 39.2 all-gather.43
  909.5 69.9 all-gather.65
  980.9 122.5 all-gather.69
  1105.0 83.2 all-gather.79
  1406.8 137.4 all-gather.71
  1545.8 83.2 all-gather.57
  1789.6 167.0 all-gather.73
  1958.2 121.4 all-gather.67
  2081.6 96.6 all-gather.81
  2179.9 102.1 all-gather.75
  2283.5 74.3 all-gather.77
  2359.5 189.4 all-gather.59
  2550.5 68.9 all-gather.83
  3121.6 114.7 all-reduce.8
